TPU v7x, 32 devices: a whole 2x2x4 slice. The times are simulated.
32 devices in a mesh: row: 4 (over z), col: 8 (over y, x, core).
Axes of the slice: x: 2, y: 2, z: 4, core: 2. Of those that a mesh axis runs over, the one named last changes fastest.
Arguments:
- factor_panel: bfloat16 [1024, 8192], P('row', 'col'), may hold values from -0.1875 to 0.1875
- ancestor_inv: float32 [1024, 1024], P('row', 'col'), may hold values from -6 to 6
- diag_inverse: float32 [4096, 8192], P('row', 'col'), may hold values from -6 to 6
- structure: int32 [2, 4], replicated, may hold values 0 or 1
Outputs:
- inverse_panel: float32 [1024, 8192], P('row', 'col')
- diag_sigma: float32 [4096, 8192], P('row', 'col')
All inputs are finite; a program needn't handle non-finite values.
Results may differ from a plain program's by a relative error of at most 0.0003.
Values may be sent and summed in bfloat16 or wider, within the bound.
A program may use at most 128 MiB of HBM per device.

v0:
```python
import jax
import jax.numpy as jnp
from jax import lax
from jax.sharding import PartitionSpec as P

B = 256
NS = 2


def local(factor_panel, ancestor_inv, diag_inverse, structure):
    rows_dev, width_dev = factor_panel.shape
    per_block = width_dev // NS
    row_index = lax.axis_index("row")
    keep_tiles = jnp.repeat(structure, B, axis=1)
    keep_own = lax.dynamic_slice_in_dim(keep_tiles, row_index * rows_dev, rows_dev, 1)
    keep_cols = jnp.repeat(keep_own.T, per_block, axis=1)
    lhat_local = jnp.where(keep_cols == 1, factor_panel, jnp.zeros_like(factor_panel))
    column = lax.all_gather(lhat_local, "row", axis=0, tiled=True)
    sigma_rows = lax.all_gather(ancestor_inv, "col", axis=1, tiled=True)
    column_wide = column.astype(jnp.float32)
    running = jnp.dot(sigma_rows, column_wide, precision=lax.Precision.HIGHEST)
    inverse_panel = jnp.where(keep_cols == 1, -running, jnp.zeros_like(running))
    rows_all = lax.all_gather(lhat_local, "col", axis=1, tiled=True)
    block_count = rows_all.shape[1] // width_dev
    rows_cube = rows_all.reshape(rows_dev, block_count, NS, per_block)
    lhat_members = [
        rows_cube[:, :, member, :].reshape(rows_dev, block_count * per_block).astype(jnp.float32)
        for member in range(NS)
    ]
    pieces = []
    for member in range(NS):
        window = lhat_members[member]
        target = inverse_panel[:, member * per_block : (member + 1) * per_block]
        pieces.append(
            lax.dot_general(
                window,
                target,
                (((0,), (0,)), ((), ())),
                precision=lax.Precision.HIGHEST,
                preferred_element_type=jnp.float32,
            )
        )
    update = lax.psum_scatter(
        jnp.concatenate(pieces, axis=1), "row", scatter_dimension=0, tiled=True
    )
    diag_sigma = diag_inverse - update
    return (inverse_panel, diag_sigma)


def solution(mesh):
    placed = (P("row", "col"), P("row", "col"), P("row", "col"), P())
    return jax.shard_map(
        local,
        mesh=mesh,
        in_specs=placed,
        out_specs=(P("row", "col"), P("row", "col")),
        check_vma=False,
    )
```

profile of v0, /device:TPU:0, one launch (start us, length us, event | category | flops | bytes accessed | tf_op | source)
XLA Modules:
  0.0 437.1 jit_solution(3430236630493984573)
XLA Ops:
  7.2 0.0 copy-start
  7.2 0.0 all-gather.6.cloned.1.call-start
  7.2 0.7 all-gather.6.cloned.1.call-update
  7.9 0.0 all-gather.4.cloned.1.call-start
  8.0 0.0 copy-done
  8.0 0.1 broadcast_bitcast_fusion
  8.1 1.2 copy.6
  9.3 0.8 bitcast_select_fusion.1
  10.2 0.0 all-gather.4.cloned.1.call-update
  10.2 0.0 all-gather.8.cloned.1.call-start
  10.2 0.7 all-gather.8.cloned.1.call-update
  10.9 0.0 reduce-scatter.2.cloned.1.call-start
  11.0 25.2 %all-gather.6.cloned.1.call-done = f32[256,1024]{1,0:T(8,128)} async-done(((f32[256,128]{1,0:T(8,128)}), f32[256,1024]{1,0:T(8,128)}) %all-gather.6.cloned.1.call-update) | async-done | bytes 1048592 | tf_op jit(solution)/shard_map/all_gather | solution.py:19
  36.2 48.4 %all-gather.4.cloned.1.call-done = bf16[1024,1024]{0,1:T(8,128)(2,1)} async-done(((bf16[256,1024]{0,1:T(8,128)(2,1)}), bf16[1024,1024]{0,1:T(8,128)(2,1)}) %all-gather.4.cloned.1.call-update) | async-done | bytes 2097168 | tf_op jit(solution)/shard_map/all_gather | solution.py:18
  84.6 3.7 bitcast_select_fusion
  88.3 33.7 %all-gather.8.cloned.1.call-done = bf16[256,8192]{0,1:T(8,128)(2,1)} async-done(((bf16[256,1024]{0,1:T(8,128)(2,1)}), bf16[256,8192]{0,1:T(8,128)(2,1)}) %all-gather.8.cloned.1.call-update) | async-done | bytes 4194320 | tf_op jit(solution)/shard_map/all_gather | solution.py:23
  122.1 2.6 fusion.5
  124.6 3.5 fusion.1
  128.1 3.5 fusion.3
  131.6 6.4 %pad_maximum_fusion = f32[4096,1024]{0,1:T(8,128)} fusion(f32[4096,512]{0,1:T(8,128)S(1)} %fusion.1, f32[4096,512]{0,1:T(8,128)S(1)} %fusion.3), kind=kLoop, calls=%fused_computation | loop fusion | flops 4194304 | bytes 33554432 | tf_op jit(solution)/shard_map/concatenate | solution.py:44
  138.0 0.0 reduce-scatter.2.cloned.1.call-update
  138.0 5.3 %copy.7 = f32[1024,1024]{0,1:T(8,128)} copy(f32[1024,1024]{1,0:T(8,128)} %param.6) | data formatting | bytes 8388608 | tf_op args[2]
  143.3 1.3 copy.8
  144.6 273.8 %reduce-scatter.2.cloned.1.call-done = f32[1024,1024]{0,1:T(8,128)} async-done(((f32[4096,1024]{0,1:T(8,128)}), f32[1024,1024]{0,1:T(8,128)}) %reduce-scatter.2.cloned.1.call-update) | async-done | bytes 4194320 | tf_op jit(solution)/shard_map/reduce_scatter | solution.py:43
  418.4 0.0 copy-start.1
  418.4 6.8 %sub.3 = f32[1024,1024]{0,1:T(8,128)} subtract(f32[1024,1024]{0,1:T(8,128)} %copy.7, f32[1024,1024]{0,1:T(8,128)} %reduce-scatter.2.cloned.1.call-done) | non-fusion elementwise | flops 1048576 | bytes 12582912 | tf_op jit(solution)/shard_map/sub | solution.py:46
  425.2 5.3 %copy.9 = f32[1024,1024]{1,0:T(8,128)} copy(f32[1024,1024]{0,1:T(8,128)} %sub.3) | data formatting | bytes 8388608
  430.6 0.0 copy-done.1
  (2 shorter events, 0.0 us)
Async XLA Ops:
  7.2 0.8 copy-start
  7.2 29.0 %all-gather.6.cloned.1.call-start = ((), (), s32[]{:S(2)}) async-start(), calls=%async_computation.2 | async-start | bytes 1179648 | tf_op jit(solution)/shard_map/all_gather | solution.py:19
  7.9 76.7 %all-gather.4.cloned.1.call-start = ((), (), s32[]{:S(2)}) async-start(), calls=%async_computation.1 | async-start | bytes 2621440 | tf_op jit(solution)/shard_map/all_gather | solution.py:18
  10.2 111.9 %all-gather.8.cloned.1.call-start = ((), (), s32[]{:S(2)}) async-start(), calls=%async_computation.3 | async-start | bytes 4718592 | tf_op jit(solution)/shard_map/all_gather | solution.py:23
  10.9 407.5 %reduce-scatter.2.cloned.1.call-start = ((), (), s32[]{:S(2)}) async-start(), calls=%async_computation.4 | async-start | bytes 20971520 | tf_op jit(solution)/shard_map/reduce_scatter | solution.py:43
  418.4 12.1 %copy-start.1 = (s32[2,4]{1,0:T(2,128)S(1)}, s32[2,4]{1,0:T(2,128)}, u32[]{:S(2)}) copy-start(s32[2,4]{1,0:T(2,128)} %param.7) | copy-start | bytes 100
Sparse Core Ops, SparseCore 0:
  9.9 26.2 all-gather.5
  38.3 46.2 all-gather.3
  87.1 34.9 all-gather.7
  138.1 280.2 reduce-scatter.1
where the time goes:
time: 437 us
  waiting for transfers between devices  383 us (88%)
  local copies, waits for them, and re-layouts  15.9 us (4%)
  other arithmetic  14 us (3%)
  between operations  13.8 us (3%)
  matrix products  10.6 us (2%)
    reduce_scatter x1, waiting for transfers between devices, local(): lax.psum_scatter(jnp.concatenate(pieces, axis=1), 'row', scatter_dimensio...  274 us
    all_gather x1, waiting for transfers between devices, local(): column = lax.all_gather(lhat_local, 'row', axis=0, tiled=True)  48.4 us
    all_gather x1, waiting for transfers between devices, local(): rows_all = lax.all_gather(lhat_local, 'col', axis=1, tiled=True)  33.7 us
    all_gather x1, waiting for transfers between devices, local(): sigma_rows = lax.all_gather(ancestor_inv, 'col', axis=1, tiled=True)  25.2 us
    unnamed x10, local copies, waits for them, and re-layouts  13.3 us
  transfers between devices with their start and end apart: 4, of which 4 were waited for; matrix products, arithmetic and copies ran while one was open for 3% of the time, Pallas kernels for 0%

commit v1 on v0

--- a/solution.py
+++ b/solution.py
@@ -20,7 +20,12 @@
     column_wide = column.astype(jnp.float32)
     running = jnp.dot(sigma_rows, column_wide, precision=lax.Precision.HIGHEST)
     inverse_panel = jnp.where(keep_cols == 1, -running, jnp.zeros_like(running))
-    rows_all = lax.all_gather(lhat_local, "col", axis=1, tiled=True)
+    ring = [lhat_local]
+    for hop in range(7):
+        ring.append(lax.ppermute(ring[-1], "col", [(dev, (dev + 1) % 8) for dev in range(8)]))
+    rows_all = jnp.roll(
+        jnp.concatenate(ring[::-1], axis=1), (lax.axis_index("col") + 1) * ring[0].shape[1], axis=1
+    )
     block_count = rows_all.shape[1] // width_dev
     rows_cube = rows_all.reshape(rows_dev, block_count, NS, per_block)
     lhat_members = [

time: 437 us -> 409 us (0.936)
  waiting for transfers between devices: 383 us -> 349 us
  local copies, waits for them, and re-layouts: 15.9 us -> 20.8 us
    ppermute x0 -> x7, waiting for transfers between devices: none -> 60 us  [local(): lax.ppermute(ring[-1], 'col', [(dev, (dev + 1) % 8) for dev in range(8)])]
    all_gather x1 -> x0, waiting for transfers between devices: 33.7 us -> none  [local(): rows_all = lax.all_gather(lhat_local, 'col', axis=1, tiled=True)]
    all_gather x1, waiting for transfers between devices: 48.4 us -> 16.2 us  [local(): column = lax.all_gather(lhat_local, 'row', axis=0, tiled=True)]
    all_gather x1, waiting for transfers between devices: 25.2 us -> 0.01 us  [local(): sigma_rows = lax.all_gather(ancestor_inv, 'col', axis=1, tiled=True)]
    unnamed x10 -> x37, local copies, waits for them, and re-layouts: 13.3 us -> 20.2 us
  transfers between devices with their start and end apart: 4 -> 10, of which waited for: 4 -> 8; matrix products, arithmetic and copies ran while one was open for 3% -> 3% of each run, Pallas kernels for 0% -> 0%
where the time goes in v1:
time: 409 us
  waiting for transfers between devices  349 us (85%)
  local copies, waits for them, and re-layouts  20.8 us (5%)
  between operations  14 us (3%)
  other arithmetic  13.4 us (3%)
  matrix products  10.7 us (3%)
    reduce_scatter x1, waiting for transfers between devices, local(): lax.psum_scatter(jnp.concatenate(pieces, axis=1), 'row', scatter_dimensio...  272 us
    ppermute x7, waiting for transfers between devices, local(): lax.ppermute(ring[-1], 'col', [(dev, (dev + 1) % 8) for dev in range(8)])  60 us
    unnamed x37, local copies, waits for them, and re-layouts  20.2 us
    all_gather x1, waiting for transfers between devices, local(): column = lax.all_gather(lhat_local, 'row', axis=0, tiled=True)  16.2 us
  transfers between devices with their start and end apart: 10, of which 8 were waited for; matrix products, arithmetic and copies ran while one was open for 3% of the time, Pallas kernels for 0%

profile of v1, /device:TPU:0, one launch (start us, length us, event | category | flops | bytes accessed | tf_op | source)
XLA Modules:
  0.0 408.5 jit_solution(14803953793508106924)
XLA Ops:
  7.2 0.0 all-gather.5.cloned.1.call-start
  7.2 0.7 all-gather.5.cloned.1.call-update
  7.9 0.0 all-gather.3.cloned.1.call-start
  8.0 0.1 broadcast_bitcast_fusion
  8.1 1.2 copy.6
  9.4 0.5 collective-permute-start
  9.9 9.7 %collective-permute-done = bf16[256,1024]{0,1:T(8,128)(2,1)S(1)} collective-permute-done((bf16[256,1024]{0,1:T(8,128)(2,1)S(1)}, bf16[256,1024]{0,1:T(8,128)(2,1)S(1)}, u32[]{:S(2)}, u32[]{:S(2)}) %collective-permute-start) | collective-permute-done | bytes 524320 | tf_op jit(solution)/shard_map/ppermute | solution.py:25
  19.6 0.0 all-gather.3.cloned.1.call-update
  19.7 0.0 reduce-scatter.2.cloned.1.call-start
  19.7 10.8 %collective-permute-done.1 = bf16[256,1024]{0,1:T(8,128)(2,1)S(1)} collective-permute-done((bf16[256,1024]{0,1:T(8,128)(2,1)S(1)}, bf16[256,1024]{0,1:T(8,128)(2,1)S(1)}, u32[]{:S(2)}, u32[]{:S(2)}) %collective-permute-start.1) | collective-permute-done | bytes 524320 | tf_op jit(solution)/shard_map/ppermute | solution.py:25
  30.6 10.9 %collective-permute-done.2 = bf16[256,1024]{0,1:T(8,128)(2,1)S(1)} collective-permute-done((bf16[256,1024]{0,1:T(8,128)(2,1)S(1)}, bf16[256,1024]{0,1:T(8,128)(2,1)S(1)}, u32[]{:S(2)}, u32[]{:S(2)}) %collective-permute-start.2) | collective-permute-done | bytes 524320 | tf_op jit(solution)/shard_map/ppermute | solution.py:25
  41.4 9.5 %collective-permute-done.3 = bf16[256,1024]{0,1:T(8,128)(2,1)S(1)} collective-permute-done((bf16[256,1024]{0,1:T(8,128)(2,1)S(1)}, bf16[256,1024]{0,1:T(8,128)(2,1)S(1)}, u32[]{:S(2)}, u32[]{:S(2)}) %collective-permute-start.3) | collective-permute-done | bytes 524320 | tf_op jit(solution)/shard_map/ppermute | solution.py:25
  50.9 9.5 %collective-permute-done.4 = bf16[256,1024]{0,1:T(8,128)(2,1)S(1)} collective-permute-done((bf16[256,1024]{0,1:T(8,128)(2,1)S(1)}, bf16[256,1024]{0,1:T(8,128)(2,1)S(1)}, u32[]{:S(2)}, u32[]{:S(2)}) %collective-permute-start.4) | collective-permute-done | bytes 524320 | tf_op jit(solution)/shard_map/ppermute | solution.py:25
  60.4 9.6 %collective-permute-done.5 = bf16[256,1024]{0,1:T(8,128)(2,1)} collective-permute-done((bf16[256,1024]{0,1:T(8,128)(2,1)S(1)}, bf16[256,1024]{0,1:T(8,128)(2,1)}, u32[]{:S(2)}, u32[]{:S(2)}) %collective-permute-start.5) | collective-permute-done | bytes 524320 | tf_op jit(solution)/shard_map/ppermute | solution.py:25
  70.1 16.2 %all-gather.3.cloned.1.call-done = bf16[1024,1024]{0,1:T(8,128)(2,1)} async-done(((bf16[256,1024]{0,1:T(8,128)(2,1)}), bf16[1024,1024]{0,1:T(8,128)(2,1)}) %all-gather.3.cloned.1.call-update) | async-done | bytes 2097168 | tf_op jit(solution)/shard_map/all_gather | solution.py:18
  86.3 3.8 bitcast_select_fusion
  90.1 1.1 constant_dynamic-update-slice_fusion.15
  91.2 1.1 constant_dynamic-update-slice_fusion.14
  92.2 1.1 constant_dynamic-update-slice_fusion.13
  93.3 1.1 constant_dynamic-update-slice_fusion.12
  94.6 1.1 constant_dynamic-update-slice_fusion.7
  95.7 1.1 constant_dynamic-update-slice_fusion.6
  97.0 0.3 constant_dynamic-slice_fusion
  97.3 0.4 fusion.5
  97.7 3.5 fusion.3
  101.2 3.5 fusion.1
  104.6 6.5 %pad_maximum_fusion = f32[4096,1024]{0,1:T(8,128)} fusion(f32[4096,512]{0,1:T(8,128)S(1)} %fusion.1, f32[4096,512]{0,1:T(8,128)S(1)} %fusion.3), kind=kLoop, calls=%fused_computation | loop fusion | flops 4194304 | bytes 33554432 | tf_op jit(solution)/shard_map/concatenate | solution.py:49
  111.2 5.3 %copy.7 = f32[1024,1024]{0,1:T(8,128)} copy(f32[1024,1024]{1,0:T(8,128)} %param.6) | data formatting | bytes 8388608 | tf_op args[2]
  116.6 1.3 copy.8
  117.9 272.0 %reduce-scatter.2.cloned.1.call-done = f32[1024,1024]{0,1:T(8,128)} async-done(((f32[4096,1024]{0,1:T(8,128)}), f32[1024,1024]{0,1:T(8,128)}) %reduce-scatter.2.cloned.1.call-update) | async-done | bytes 4194320 | tf_op jit(solution)/shard_map/reduce_scatter | solution.py:48
  389.9 6.8 %sub.8 = f32[1024,1024]{0,1:T(8,128)} subtract(f32[1024,1024]{0,1:T(8,128)} %copy.7, f32[1024,1024]{0,1:T(8,128)} %reduce-scatter.2.cloned.1.call-done) | non-fusion elementwise | flops 1048576 | bytes 12582912 | tf_op jit(solution)/shard_map/sub | solution.py:51
  396.7 5.3 %copy.9 = f32[1024,1024]{1,0:T(8,128)} copy(f32[1024,1024]{0,1:T(8,128)} %sub.8) | data formatting | bytes 8388608
  (38 shorter events, 0.5 us)
Async XLA Ops:
  7.2 0.8 copy-start
  7.2 62.9 %all-gather.5.cloned.1.call-start = ((), (), s32[]{:S(2)}) async-start(), calls=%async_computation.2 | async-start | bytes 1179648 | tf_op jit(solution)/shard_map/all_gather | solution.py:19
  7.9 78.3 %all-gather.3.cloned.1.call-start = ((), (), s32[]{:S(2)}) async-start(), calls=%async_computation.1 | async-start | bytes 2621440 | tf_op jit(solution)/shard_map/all_gather | solution.py:18
  9.4 10.3 %copy-start.2 = (bf16[256,1024]{0,1:T(8,128)(2,1)}, bf16[256,1024]{0,1:T(8,128)(2,1)S(1)}, u32[]{:S(2)}) copy-start(bf16[256,1024]{0,1:T(8,128)(2,1)S(1)} %bitcast_select_fusion.1) | copy-start | bytes 1572868
  9.4 10.3 %collective-permute-start = (bf16[256,1024]{0,1:T(8,128)(2,1)S(1)}, bf16[256,1024]{0,1:T(8,128)(2,1)S(1)}, u32[]{:S(2)}, u32[]{:S(2)}) collective-permute-start(bf16[256,1024]{0,1:T(8,128)(2,1)S(1)} %bitcast_select_fusion.1), channel_id=1, source_target_pairs={{0,1},{1,2},{2,3},{3,4},{4,5},{5,6},{6,7},{7,0},{8,9},{9,10},{10,1... | collective-permute-start | bytes 1572872 | tf_op jit(solution)/shard_map/ppermute | solution.py:25
  19.6 10.9 %collective-permute-start.1 = (bf16[256,1024]{0,1:T(8,128)(2,1)S(1)}, bf16[256,1024]{0,1:T(8,128)(2,1)S(1)}, u32[]{:S(2)}, u32[]{:S(2)}) collective-permute-start(bf16[256,1024]{0,1:T(8,128)(2,1)S(1)} %collective-permute-done), channel_id=1, source_target_pairs={{0,1},{1,2},{2,3},{3,4},{4,5},{5,6},{6,7},{7,0},{8,9},{9,10},{10,1... | collective-permute-start | bytes 1572872 | tf_op jit(solution)/shard_map/ppermute | solution.py:25
  19.7 74.9 %copy-start.3 = (bf16[256,1024]{0,1:T(8,128)(2,1)S(1)}, bf16[256,1024]{0,1:T(8,128)(2,1)}, u32[]{:S(2)}) copy-start(bf16[256,1024]{0,1:T(8,128)(2,1)} %copy-done.2) | copy-start | bytes 1572868
  19.7 370.2 %reduce-scatter.2.cloned.1.call-start = ((), (), s32[]{:S(2)}) async-start(), calls=%async_computation.3 | async-start | bytes 20971520 | tf_op jit(solution)/shard_map/reduce_scatter | solution.py:48
  30.6 10.9 %collective-permute-start.2 = (bf16[256,1024]{0,1:T(8,128)(2,1)S(1)}, bf16[256,1024]{0,1:T(8,128)(2,1)S(1)}, u32[]{:S(2)}, u32[]{:S(2)}) collective-permute-start(bf16[256,1024]{0,1:T(8,128)(2,1)S(1)} %collective-permute-done.1), channel_id=1, source_target_pairs={{0,1},{1,2},{2,3},{3,4},{4,5},{5,6},{6,7},{7,0},{8,9},{9,10},{10,1... | collective-permute-start | bytes 1572872 | tf_op jit(solution)/shard_map/ppermute | solution.py:25
  41.4 9.5 %collective-permute-start.3 = (bf16[256,1024]{0,1:T(8,128)(2,1)S(1)}, bf16[256,1024]{0,1:T(8,128)(2,1)S(1)}, u32[]{:S(2)}, u32[]{:S(2)}) collective-permute-start(bf16[256,1024]{0,1:T(8,128)(2,1)S(1)} %collective-permute-done.2), channel_id=1, source_target_pairs={{0,1},{1,2},{2,3},{3,4},{4,5},{5,6},{6,7},{7,0},{8,9},{9,10},{10,1... | collective-permute-start | bytes 1572872 | tf_op jit(solution)/shard_map/ppermute | solution.py:25
  50.9 19.1 %copy-start.4 = (bf16[256,1024]{0,1:T(8,128)(2,1)}, bf16[256,1024]{0,1:T(8,128)(2,1)S(1)}, u32[]{:S(2)}) copy-start(bf16[256,1024]{0,1:T(8,128)(2,1)S(1)} %collective-permute-done.3) | copy-start | bytes 1572868
  50.9 9.5 %collective-permute-start.4 = (bf16[256,1024]{0,1:T(8,128)(2,1)S(1)}, bf16[256,1024]{0,1:T(8,128)(2,1)S(1)}, u32[]{:S(2)}, u32[]{:S(2)}) collective-permute-start(bf16[256,1024]{0,1:T(8,128)(2,1)S(1)} %collective-permute-done.3), channel_id=1, source_target_pairs={{0,1},{1,2},{2,3},{3,4},{4,5},{5,6},{6,7},{7,0},{8,9},{9,10},{10,1... | collective-permute-start | bytes 1572872 | tf_op jit(solution)/shard_map/ppermute | solution.py:25
  60.4 9.6 %copy-start.6 = (bf16[256,1024]{0,1:T(8,128)(2,1)}, bf16[256,1024]{0,1:T(8,128)(2,1)S(1)}, u32[]{:S(2)}) copy-start(bf16[256,1024]{0,1:T(8,128)(2,1)S(1)} %collective-permute-done.4) | copy-start | bytes 1572868
  60.4 9.6 %collective-permute-start.5 = (bf16[256,1024]{0,1:T(8,128)(2,1)S(1)}, bf16[256,1024]{0,1:T(8,128)(2,1)}, u32[]{:S(2)}, u32[]{:S(2)}) collective-permute-start(bf16[256,1024]{0,1:T(8,128)(2,1)S(1)} %collective-permute-done.4), channel_id=1, source_target_pairs={{0,1},{1,2},{2,3},{3,4},{4,5},{5,6},{6,7},{7,0},{8,9},{9,10},{10,1... | collective-permute-start | bytes 1572872 | tf_op jit(solution)/shard_map/ppermute | solution.py:25
  70.0 20.0 %collective-permute-start.6 = (bf16[256,1024]{0,1:T(8,128)(2,1)}, bf16[256,1024]{0,1:T(8,128)(2,1)}, u32[]{:S(2)}, u32[]{:S(2)}) collective-permute-start(bf16[256,1024]{0,1:T(8,128)(2,1)} %collective-permute-done.5), channel_id=1, source_target_pairs={{0,1},{1,2},{2,3},{3,4},{4,5},{5,6},{6,7},{7,0},{8,9},{9,10},{10,1... | collective-permute-start | bytes 1572872 | tf_op jit(solution)/shard_map/ppermute | solution.py:25
  86.3 10.5 %copy-start.7 = (bf16[256,1024]{0,1:T(8,128)(2,1)S(1)}, bf16[256,1024]{0,1:T(8,128)(2,1)}, u32[]{:S(2)}) copy-start(bf16[256,1024]{0,1:T(8,128)(2,1)} %copy-done.6) | copy-start | bytes 1572868
  86.3 10.6 %copy-start.5 = (bf16[256,1024]{0,1:T(8,128)(2,1)S(1)}, bf16[256,1024]{0,1:T(8,128)(2,1)}, u32[]{:S(2)}) copy-start(bf16[256,1024]{0,1:T(8,128)(2,1)} %copy-done.4) | copy-start | bytes 1572868
  116.6 285.5 %copy-start.1 = (s32[2,4]{1,0:T(2,128)S(1)}, s32[2,4]{1,0:T(2,128)}, u32[]{:S(2)}) copy-start(s32[2,4]{1,0:T(2,128)} %param.7) | copy-start | bytes 100
Sparse Core Ops, SparseCore 0:
  9.9 27.1 all-gather.4
  39.3 46.9 all-gather.2
  111.3 278.5 reduce-scatter.1
